TPU v7x, 32 devices: a whole 2x2x4 slice. The times are simulated.
32 devices in a mesh: grp: 4 (over z), mem: 8 (over y, x, core).
Axes of the slice: x: 2, y: 2, z: 4, core: 2. Of those that a mesh axis runs over, the one named last changes fastest.
Arguments:
- basis: float32 [20, 2048, 128], P(None, ('grp', 'mem'))
- precond: bfloat16 [2048, 128, 128], P(('grp', 'mem'))
- leaf_rows: float32 [1024, 128], P(('grp', 'mem')), may hold values from -6 to 6
- leaf_fiber: int32 [1024], P(('grp', 'mem')), may hold values from 0 to 63
- strad_rows: float32 [1024, 128], P(('grp', 'mem')), may hold values from -6 to 6
- strad_fiber: int32 [1024], P(('grp', 'mem')), may hold values from 0 to 63
- strad_count: int32 [32, 4], P(('grp', 'mem')), may hold values from 0 to 8, as said below
Outputs:
- coeffs: float32 [21], replicated
- next_vector: float32 [2048, 128], P(('grp', 'mem'))
Inputs may be any that keep to these rules, and one draw needn't show every extreme that they name: `leaf_fiber`: a destination fiber within the destination device. `strad_fiber`: a fiber of the receiving device. The first strad_count slots of a block are live, the rest are not read; some device fills a block.
All inputs are finite; a program needn't handle non-finite values.
Results may differ from a plain program's by a relative error of at most 0.0011.
Values sent between devices are 32-bit elements; how exact they have to be, the bound alone decides.
A program may use at most 64 MiB of HBM per device.

v0:
```python
import jax
import jax.numpy as jnp
from jax import lax
from jax.sharding import PartitionSpec as P

EPS = 1e-06


def local(basis, precond, leaf_rows, leaf_fiber, strad_rows, strad_fiber, strad_count):
    groups = lax.axis_size("grp")
    members = lax.axis_size("mem")
    krylov, fibers_here, width = basis.shape
    fiber_index = jnp.arange(fibers_here, dtype=jnp.int32)
    arrived, arrived_ids = (
        lax.all_to_all(leaf_rows, "mem", split_axis=0, concat_axis=0, tiled=True),
        lax.all_to_all(
            leaf_fiber.astype(jnp.float32), "mem", split_axis=0, concat_axis=0, tiled=True
        ),
    )
    select = (fiber_index[:, None] == arrived_ids.astype(jnp.int32)[None, :]).astype(jnp.float32)
    far_field = jnp.dot(
        select, arrived, precision=lax.Precision.HIGHEST, preferred_element_type=jnp.float32
    )
    strad_slots = strad_rows.shape[0] // groups
    keeping = (jnp.arange(strad_slots, dtype=jnp.int32)[None, :] < strad_count[0][:, None]).reshape(
        -1
    )
    outgoing = strad_rows * keeping[:, None].astype(jnp.float32)
    incoming = lax.all_to_all(outgoing, "grp", split_axis=0, concat_axis=0, tiled=True)
    select_near = (fiber_index[:, None] == strad_fiber[None, :]).astype(jnp.float32)
    near_field = jnp.dot(
        select_near, incoming, precision=lax.Precision.HIGHEST, preferred_element_type=jnp.float32
    )
    field = (basis[krylov - 1] + far_field + near_field).astype(jnp.bfloat16)
    applied = jnp.einsum("fij,fj->fi", precond, field, preferred_element_type=jnp.float32)
    total = float(fibers_here * width * groups * members)
    local_coef = jnp.einsum("kfi,fi->k", basis, applied, precision=lax.Precision.HIGHEST)
    gram_local = jnp.einsum("kfi,lfi->kl", basis, basis, precision=lax.Precision.HIGHEST)
    coef_sum, square_sum, gram_sum = lax.psum(
        (local_coef, jnp.sum(applied * applied), gram_local), ("grp", "mem")
    )
    coef = coef_sum / total
    gram = gram_sum / total
    residual = applied - jnp.einsum("k,kfi->fi", coef, basis, precision=lax.Precision.HIGHEST)
    projected = jnp.dot(gram, coef, precision=lax.Precision.HIGHEST)
    square = square_sum / total - 2.0 * jnp.sum(coef * coef) + jnp.sum(coef * projected)
    beta = jnp.sqrt(square + EPS)
    return (jnp.concatenate([coef, beta[None]]), residual / beta)


def solution(mesh):
    return jax.shard_map(
        local,
        mesh=mesh,
        in_specs=(
            P(None, ("grp", "mem"), None),
            P(("grp", "mem"), None, None),
            P(("grp", "mem"), None),
            P(("grp", "mem")),
            P(("grp", "mem"), None),
            P(("grp", "mem")),
            P(("grp", "mem"), None),
        ),
        out_specs=(P(), P(("grp", "mem"), None)),
        check_vma=False,
    )
```

profile of v0, /device:TPU:0, one launch (start us, length us, event | category | flops | bytes accessed | tf_op | source)
XLA Modules:
  0.0 79.5 jit_solution(3475346898591158441)
XLA Ops:
  0.6 0.0 copy-start
  0.7 0.8 %convert_element_type.29 = f32[32]{0:T(128)S(1)} convert(s32[32]{0:T(128)} %param.10) | non-fusion elementwise | flops 32 | bytes 256 | tf_op jit(solution)/shard_map/convert_element_type | solution.py:17
  1.5 0.7 all_to_all.22
  2.1 5.2 %all-to-all-start = ((f32[8,4,1]{1,2,0:T(1,128)}), f32[8,4,1]{1,2,0:T(1,128)S(1)}, u32[]{:S(2)}, u32[]{:S(2)}) async-start(f32[8,4,1]{1,2,0:T(1,128)} %bitcast.1), calls=%async_computation | async-start | bytes 8192 | tf_op jit(solution)/shard_map/all_to_all | solution.py:16
  7.3 0.7 fusion.16
  8.1 0.1 reshape.35
  8.2 1.4 %multiply_bitcast_fusion = f32[4,8,128]{2,1,0:T(8,128)} fusion(f32[32,128]{1,0:T(8,128)} %param.11, f32[32]{0:T(128)S(1)} %reshape.35), kind=kLoop, calls=%fused_computation.21 | loop fusion | flops 4096 | bytes 32896 | tf_op jit(solution)/shard_map/all_to_all | solution.py:29
  9.5 2.8 %convolution_bitcast_fusion = f32[20,20]{1,0:T(8,128)S(1)} fusion(f32[20,64,128]{2,1,0:T(8,128)} %param.7), kind=kOutput, calls=%fused_computation.4 | convolution fusion | flops 39321600 | bytes 656960 | tf_op jit(solution)/shard_map/kfi,lfi->kl/dot_general | solution.py:38
  12.3 4.2 %all-to-all-start.1 = ((f32[8,4,128]{2,1,0:T(4,128)}), f32[8,4,128]{2,1,0:T(4,128)S(1)}, u32[]{:S(2)}, u32[]{:S(2)}) async-start(f32[8,4,128]{2,1,0:T(4,128)} %bitcast.45), calls=%async_computation.1 | async-start | bytes 32768 | tf_op jit(solution)/shard_map/all_to_all | solution.py:15
  16.5 0.1 convert_element_type.31
  16.6 4.7 %all-to-all-done.1 = f32[8,4,128]{2,1,0:T(4,128)S(1)} async-done(((f32[8,4,128]{2,1,0:T(4,128)}), f32[8,4,128]{2,1,0:T(4,128)S(1)}, u32[]{:S(2)}, u32[]{:S(2)}) %all-to-all-start.1) | async-done | bytes 16416 | tf_op jit(solution)/shard_map/all_to_all | solution.py:15
  21.3 4.9 %all-to-all-start.2 = ((f32[4,8,128]{2,1,0:T(8,128)}), f32[4,8,128]{2,1,0:T(8,128)S(1)}, u32[]{:S(2)}, u32[]{:S(2)}) async-start(f32[4,8,128]{2,1,0:T(8,128)} %multiply_bitcast_fusion), calls=%async_computation.2 | async-start | bytes 32768 | tf_op jit(solution)/shard_map/all_to_all | solution.py:29
  26.2 0.9 %convolution_add_fusion.1 = f32[64,128]{1,0:T(8,128)S(1)} fusion(f32[32,128]{1,0:T(8,128)S(1)} %bitcast.44, f32[20,64,128]{2,1,0:T(8,128)} %param.7, s32[32]{0:T(128)S(1)} %convert_element_type.31), kind=kOutput, calls=%fused_computation.1 | convolution fusion | flops 3155968 | bytes 82048 | tf_op jit(solution)/shard_map/dot_general | solution.py:21
  27.1 4.7 %all-to-all-done.2 = f32[4,8,128]{2,1,0:T(8,128)S(1)} async-done(((f32[4,8,128]{2,1,0:T(8,128)}), f32[4,8,128]{2,1,0:T(8,128)S(1)}, u32[]{:S(2)}, u32[]{:S(2)}) %all-to-all-start.2) | async-done | bytes 16416 | tf_op jit(solution)/shard_map/all_to_all | solution.py:29
  31.8 0.8 %fusion.1 = bf16[64,128,1]{1,0,2:T(8,128)(2,1)S(1)} fusion(f32[64,128]{1,0:T(8,128)S(1)} %convolution_add_fusion.1, f32[4,8,128]{2,1,0:T(8,128)S(1)} %all-to-all-done.2, s32[32]{0:T(128)} %param.12), kind=kOutput, calls=%fused_computation.3 | convolution fusion | flops 3164160 | bytes 65664 | tf_op jit(solution)/shard_map/dot_general | solution.py:31
  32.6 1.2 %fusion.9 = f32[64,1,128]{2,1,0:T(1,128)S(1)} fusion(bf16[64,128,128]{2,1,0:T(8,128)(2,1)S(1)} %copy-done, bf16[64,128,1]{1,0,2:T(8,128)(2,1)S(1)} %fusion.1), kind=kOutput, calls=%fused_computation.14 | convolution fusion | flops 2097152 | bytes 2146304 | tf_op jit(solution)/shard_map/fij,fj->fi/dot_general | solution.py:35
  33.8 1.1 %convolution_bitcast_fusion.2 = f32[20]{0:T(128)S(1)} fusion(f32[20,64,128]{2,1,0:T(8,128)S(1)} %copy-done.1, f32[64,1,128]{2,1,0:T(1,128)S(1)} %fusion.9), kind=kOutput, calls=%fused_computation.7 | convolution fusion | flops 1966080 | bytes 688208 | tf_op jit(solution)/shard_map/kfi,fi->k/dot_general | solution.py:37
  34.8 0.6 multiply_reduce_fusion
  35.5 38.5 %all-reduce = (f32[]{:T(128)}, f32[20]{0:T(128)S(1)}, f32[20,20]{1,0:T(8,128)S(1)}) all-reduce(f32[]{:T(128)} %multiply_reduce_fusion, f32[20]{0:T(128)S(1)} %convolution_bitcast_fusion.2, f32[20,20]{1,0:T(8,128)S(1)} %convolution_bitcast_fusion), channel_id=1, replica_groups=mesh['grp'=4,'mem'=8] {'grp','mem'}, use_global_device_ids=true, to_apply=%region_2.0 | all-reduce | flops 421 | bytes 3368 | tf_op jit(solution)/shard_map/psum | solution.py:39
  74.0 0.6 broadcast_multiply_fusion
  74.6 0.9 %fusion.3 = f32[1,64,128]{2,0,1:T(1,128)S(1)} fusion(f32[20,64,128]{2,1,0:T(8,128)S(1)} %copy-done.1, f32[20]{0:T(128)S(1)} %get-tuple-element.3), kind=kOutput, calls=%fused_computation.8 | convolution fusion | flops 1966100 | bytes 688208 | tf_op jit(solution)/shard_map/k,kfi->fi/dot_general | solution.py:44
  75.5 0.8 %fusion.7 = f32[]{:T(128)} fusion(f32[20,20]{1,0:T(8,128)S(1)} %get-tuple-element.4, f32[20]{0:T(128)S(1)} %get-tuple-element.3), kind=kOutput, calls=%fused_computation.12 | convolution fusion | flops 5279 | bytes 1684 | tf_op jit(solution)/shard_map/dot_general | solution.py:45
  78.3 0.6 subtract_divide_fusion
  78.9 0.6 pad_maximum_fusion
  (5 shorter events, 0.0 us)
Async XLA Ops:
  0.6 31.9 %copy-start = (bf16[64,128,128]{2,1,0:T(8,128)(2,1)S(1)}, bf16[64,128,128]{2,1,0:T(8,128)(2,1)}, u32[]{:S(2)}) copy-start(bf16[64,128,128]{2,1,0:T(8,128)(2,1)} %param.8) | copy-start | bytes 6291460
  0.6 33.1 %copy-start.1 = (f32[20,64,128]{2,1,0:T(8,128)S(1)}, f32[20,64,128]{2,1,0:T(8,128)}, u32[]{:S(2)}) copy-start(f32[20,64,128]{2,1,0:T(8,128)} %param.7) | copy-start | bytes 1966084
  2.1 10.2 %all-to-all-start = ((f32[8,4,1]{1,2,0:T(1,128)}), f32[8,4,1]{1,2,0:T(1,128)S(1)}, u32[]{:S(2)}, u32[]{:S(2)}) async-start(f32[8,4,1]{1,2,0:T(1,128)} %bitcast.1), calls=%async_computation | async-start | bytes 8192 | tf_op jit(solution)/shard_map/all_to_all | solution.py:16
  12.3 9.0 %all-to-all-start.1 = ((f32[8,4,128]{2,1,0:T(4,128)}), f32[8,4,128]{2,1,0:T(4,128)S(1)}, u32[]{:S(2)}, u32[]{:S(2)}) async-start(f32[8,4,128]{2,1,0:T(4,128)} %bitcast.45), calls=%async_computation.1 | async-start | bytes 32768 | tf_op jit(solution)/shard_map/all_to_all | solution.py:15
  21.3 10.5 %all-to-all-start.2 = ((f32[4,8,128]{2,1,0:T(8,128)}), f32[4,8,128]{2,1,0:T(8,128)S(1)}, u32[]{:S(2)}, u32[]{:S(2)}) async-start(f32[4,8,128]{2,1,0:T(8,128)} %multiply_bitcast_fusion), calls=%async_computation.2 | async-start | bytes 32768 | tf_op jit(solution)/shard_map/all_to_all | solution.py:29
where the time goes:
time: 80.1 us; the launch traced here: 79.5 us
  blocking collectives  38.5 us (48%)
  starting transfers between devices  14.3 us (18%)
  waiting for transfers between devices  9.37 us (12%)
  matrix products  8.4 us (10%)
  other arithmetic  5.37 us (7%)
  between operations  2.73 us (3%)
  local copies, waits for them, and re-layouts  0.86 us (1%)
    psum x1, blocking collectives, local(): lax.psum((local_coef, jnp.sum(applied * applied), gram_local), ('grp', 'm...  38.5 us
    all_to_all x1, starting transfers between devices, local(): lax.all_to_all(leaf_fiber.astype(jnp.float32), 'mem', split_axis=0, conca...  5.2 us
    all_to_all x1, starting transfers between devices, local(): lax.all_to_all(outgoing, 'grp', split_axis=0, concat_axis=0, tiled=True)  4.88 us
    all_to_all x1, waiting for transfers between devices, local(): lax.all_to_all(outgoing, 'grp', split_axis=0, concat_axis=0, tiled=True)  4.71 us
    all_to_all x1, waiting for transfers between devices, local(): lax.all_to_all(leaf_rows, 'mem', split_axis=0, concat_axis=0, tiled=True)  4.65 us
    all_to_all x1, starting transfers between devices, local(): lax.all_to_all(leaf_rows, 'mem', split_axis=0, concat_axis=0, tiled=True)  4.21 us
    dot_general x1, matrix products, local(): jnp.einsum('kfi,lfi->kl', basis, basis, precision=lax.Precision.HIGHEST)  2.75 us
  transfers between devices with their start and end apart: 3, of which 2 were waited for; matrix products, arithmetic and copies ran while one was open for 7% of the time, Pallas kernels for 0%

commit v1 on v0

--- a/solution.py
+++ b/solution.py
@@ -7,6 +7,10 @@
 
 
 def local(basis, precond, leaf_rows, leaf_fiber, strad_rows, strad_fiber, strad_count):
+
+    def treat_stocks_all(slab_in):
+        return lax.psum(lax.psum(slab_in, "grp"), "mem")
+
     groups = lax.axis_size("grp")
     members = lax.axis_size("mem")
     krylov, fibers_here, width = basis.shape
@@ -36,8 +40,8 @@
     total = float(fibers_here * width * groups * members)
     local_coef = jnp.einsum("kfi,fi->k", basis, applied, precision=lax.Precision.HIGHEST)
     gram_local = jnp.einsum("kfi,lfi->kl", basis, basis, precision=lax.Precision.HIGHEST)
-    coef_sum, square_sum, gram_sum = lax.psum(
-        (local_coef, jnp.sum(applied * applied), gram_local), ("grp", "mem")
+    coef_sum, square_sum, gram_sum = treat_stocks_all(
+        (local_coef, jnp.sum(applied * applied), gram_local)
     )
     coef = coef_sum / total
     gram = gram_sum / total

time: 80.1 us -> 82.1 us (1.025)
  blocking collectives: 38.5 us -> 40.5 us
    psum x1 -> x2, blocking collectives: 38.5 us -> 40.5 us  [treat_stocks_all(): return lax.psum(lax.psum(slab_in, 'grp'), 'mem')]
where the time goes in v1:
time: 82.1 us; the launch traced here: 81.5 us
  blocking collectives  40.5 us (49%)
  starting transfers between devices  14.3 us (17%)
  waiting for transfers between devices  9.37 us (11%)
  matrix products  8.4 us (10%)
  other arithmetic  5.37 us (7%)
  between operations  2.73 us (3%)
  local copies, waits for them, and re-layouts  0.86 us (1%)
    psum x2, blocking collectives, treat_stocks_all(): return lax.psum(lax.psum(slab_in, 'grp'), 'mem')  40.5 us
    all_to_all x1, starting transfers between devices, local(): lax.all_to_all(leaf_fiber.astype(jnp.float32), 'mem', split_axis=0, conca...  5.2 us
    all_to_all x1, starting transfers between devices, local(): lax.all_to_all(outgoing, 'grp', split_axis=0, concat_axis=0, tiled=True)  4.88 us
    all_to_all x1, waiting for transfers between devices, local(): lax.all_to_all(outgoing, 'grp', split_axis=0, concat_axis=0, tiled=True)  4.71 us
    all_to_all x1, waiting for transfers between devices, local(): lax.all_to_all(leaf_rows, 'mem', split_axis=0, concat_axis=0, tiled=True)  4.65 us
    all_to_all x1, starting transfers between devices, local(): lax.all_to_all(leaf_rows, 'mem', split_axis=0, concat_axis=0, tiled=True)  4.21 us
    dot_general x1, matrix products, local(): jnp.einsum('kfi,lfi->kl', basis, basis, precision=lax.Precision.HIGHEST)  2.75 us
  transfers between devices with their start and end apart: 3, of which 2 were waited for; matrix products, arithmetic and copies ran while one was open for 7% of the time, Pallas kernels for 0%

profile of v1, /device:TPU:0, one launch (start us, length us, event | category | flops | bytes accessed | tf_op | source)
XLA Modules:
  0.0 81.5 jit_solution(2610280801536276341)
XLA Ops:
  0.7 0.8 convert_element_type.29
  1.5 0.7 all_to_all.22
  2.1 5.2 %all-to-all-start = ((f32[8,4,1]{1,2,0:T(1,128)}), f32[8,4,1]{1,2,0:T(1,128)S(1)}, u32[]{:S(2)}, u32[]{:S(2)}) async-start(f32[8,4,1]{1,2,0:T(1,128)} %bitcast.1), calls=%async_computation | async-start | bytes 8192 | tf_op jit(solution)/shard_map/all_to_all | solution.py:20
  7.3 0.7 fusion.16
  8.1 0.1 reshape.35
  8.2 1.4 %multiply_bitcast_fusion = f32[4,8,128]{2,1,0:T(8,128)} fusion(f32[32,128]{1,0:T(8,128)} %param.11, f32[32]{0:T(128)S(1)} %reshape.35), kind=kLoop, calls=%fused_computation.21 | loop fusion | flops 4096 | bytes 32896 | tf_op jit(solution)/shard_map/all_to_all | solution.py:33
  9.5 2.8 %convolution_bitcast_fusion = f32[20,20]{1,0:T(8,128)S(1)} fusion(f32[20,64,128]{2,1,0:T(8,128)} %param.7), kind=kOutput, calls=%fused_computation.4 | convolution fusion | flops 39321600 | bytes 656960 | tf_op jit(solution)/shard_map/kfi,lfi->kl/dot_general | solution.py:42
  12.3 4.2 %all-to-all-start.1 = ((f32[8,4,128]{2,1,0:T(4,128)}), f32[8,4,128]{2,1,0:T(4,128)S(1)}, u32[]{:S(2)}, u32[]{:S(2)}) async-start(f32[8,4,128]{2,1,0:T(4,128)} %bitcast.45), calls=%async_computation.1 | async-start | bytes 32768 | tf_op jit(solution)/shard_map/all_to_all | solution.py:19
  16.5 0.1 convert_element_type.31
  16.6 4.7 %all-to-all-done.1 = f32[8,4,128]{2,1,0:T(4,128)S(1)} async-done(((f32[8,4,128]{2,1,0:T(4,128)}), f32[8,4,128]{2,1,0:T(4,128)S(1)}, u32[]{:S(2)}, u32[]{:S(2)}) %all-to-all-start.1) | async-done | bytes 16416 | tf_op jit(solution)/shard_map/all_to_all | solution.py:19
  21.3 4.9 %all-to-all-start.2 = ((f32[4,8,128]{2,1,0:T(8,128)}), f32[4,8,128]{2,1,0:T(8,128)S(1)}, u32[]{:S(2)}, u32[]{:S(2)}) async-start(f32[4,8,128]{2,1,0:T(8,128)} %multiply_bitcast_fusion), calls=%async_computation.2 | async-start | bytes 32768 | tf_op jit(solution)/shard_map/all_to_all | solution.py:33
  26.2 0.9 %convolution_add_fusion.1 = f32[64,128]{1,0:T(8,128)S(1)} fusion(f32[32,128]{1,0:T(8,128)S(1)} %bitcast.44, f32[20,64,128]{2,1,0:T(8,128)} %param.7, s32[32]{0:T(128)S(1)} %convert_element_type.31), kind=kOutput, calls=%fused_computation.1 | convolution fusion | flops 3155968 | bytes 82048 | tf_op jit(solution)/shard_map/dot_general | solution.py:25
  27.1 4.7 %all-to-all-done.2 = f32[4,8,128]{2,1,0:T(8,128)S(1)} async-done(((f32[4,8,128]{2,1,0:T(8,128)}), f32[4,8,128]{2,1,0:T(8,128)S(1)}, u32[]{:S(2)}, u32[]{:S(2)}) %all-to-all-start.2) | async-done | bytes 16416 | tf_op jit(solution)/shard_map/all_to_all | solution.py:33
  31.8 0.8 fusion.1
  32.6 1.2 %fusion.9 = f32[64,1,128]{2,1,0:T(1,128)S(1)} fusion(bf16[64,128,128]{2,1,0:T(8,128)(2,1)S(1)} %copy-done, bf16[64,128,1]{1,0,2:T(8,128)(2,1)S(1)} %fusion.1), kind=kOutput, calls=%fused_computation.14 | convolution fusion | flops 2097152 | bytes 2146304 | tf_op jit(solution)/shard_map/fij,fj->fi/dot_general | solution.py:39
  33.8 1.1 %convolution_bitcast_fusion.2 = f32[20]{0:T(128)S(1)} fusion(f32[20,64,128]{2,1,0:T(8,128)S(1)} %copy-done.1, f32[64,1,128]{2,1,0:T(1,128)S(1)} %fusion.9), kind=kOutput, calls=%fused_computation.7 | convolution fusion | flops 1966080 | bytes 688208 | tf_op jit(solution)/shard_map/kfi,fi->k/dot_general | solution.py:41
  34.8 0.6 multiply_reduce_fusion
  35.5 17.1 %all-reduce.1 = (f32[]{:T(128)}, f32[20]{0:T(128)S(1)}, f32[20,20]{1,0:T(8,128)S(1)}) all-reduce(f32[]{:T(128)} %multiply_reduce_fusion, f32[20]{0:T(128)S(1)} %convolution_bitcast_fusion.2, f32[20,20]{1,0:T(8,128)S(1)} %convolution_bitcast_fusion), channel_id=1, replica_groups=mesh['grp'=4,'mem'=8] {'grp'}, use_global_device_ids=true, to_apply=%region_3.0 | all-reduce | flops 421 | bytes 3368 | tf_op jit(solution)/shard_map/psum | solution.py:12
  52.6 23.4 %all-reduce = (f32[]{:T(128)}, f32[20]{0:T(128)S(1)}, f32[20,20]{1,0:T(8,128)S(1)}) all-reduce(f32[]{:T(128)} %get-tuple-element.5, f32[20]{0:T(128)S(1)} %get-tuple-element.6, f32[20,20]{1,0:T(8,128)S(1)} %get-tuple-element.7), channel_id=1, replica_groups=mesh['grp'=4,'mem'=8] {'mem'}, use_global_device_ids=true, to_apply=%region_4.0 | all-reduce | flops 421 | bytes 3368 | tf_op jit(solution)/shard_map/psum | solution.py:12
  76.0 0.6 broadcast_multiply_fusion
  76.6 0.9 %fusion.3 = f32[1,64,128]{2,0,1:T(1,128)S(1)} fusion(f32[20,64,128]{2,1,0:T(8,128)S(1)} %copy-done.1, f32[20]{0:T(128)S(1)} %get-tuple-element.3), kind=kOutput, calls=%fused_computation.8 | convolution fusion | flops 1966100 | bytes 688208 | tf_op jit(solution)/shard_map/k,kfi->fi/dot_general | solution.py:48
  77.5 0.8 %fusion.7 = f32[]{:T(128)} fusion(f32[20,20]{1,0:T(8,128)S(1)} %get-tuple-element.4, f32[20]{0:T(128)S(1)} %get-tuple-element.3), kind=kOutput, calls=%fused_computation.12 | convolution fusion | flops 5279 | bytes 1684 | tf_op jit(solution)/shard_map/dot_general | solution.py:49
  80.3 0.6 subtract_divide_fusion
  80.9 0.6 pad_maximum_fusion
  (6 shorter events, 0.0 us)
Async XLA Ops:
  0.6 31.9 %copy-start = (bf16[64,128,128]{2,1,0:T(8,128)(2,1)S(1)}, bf16[64,128,128]{2,1,0:T(8,128)(2,1)}, u32[]{:S(2)}) copy-start(bf16[64,128,128]{2,1,0:T(8,128)(2,1)} %param.8) | copy-start | bytes 6291460
  0.6 33.1 %copy-start.1 = (f32[20,64,128]{2,1,0:T(8,128)S(1)}, f32[20,64,128]{2,1,0:T(8,128)}, u32[]{:S(2)}) copy-start(f32[20,64,128]{2,1,0:T(8,128)} %param.7) | copy-start | bytes 1966084
  2.1 10.2 %all-to-all-start = ((f32[8,4,1]{1,2,0:T(1,128)}), f32[8,4,1]{1,2,0:T(1,128)S(1)}, u32[]{:S(2)}, u32[]{:S(2)}) async-start(f32[8,4,1]{1,2,0:T(1,128)} %bitcast.1), calls=%async_computation | async-start | bytes 8192 | tf_op jit(solution)/shard_map/all_to_all | solution.py:20
  12.3 9.0 %all-to-all-start.1 = ((f32[8,4,128]{2,1,0:T(4,128)}), f32[8,4,128]{2,1,0:T(4,128)S(1)}, u32[]{:S(2)}, u32[]{:S(2)}) async-start(f32[8,4,128]{2,1,0:T(4,128)} %bitcast.45), calls=%async_computation.1 | async-start | bytes 32768 | tf_op jit(solution)/shard_map/all_to_all | solution.py:19
  21.3 10.5 %all-to-all-start.2 = ((f32[4,8,128]{2,1,0:T(8,128)}), f32[4,8,128]{2,1,0:T(8,128)S(1)}, u32[]{:S(2)}, u32[]{:S(2)}) async-start(f32[4,8,128]{2,1,0:T(8,128)} %multiply_bitcast_fusion), calls=%async_computation.2 | async-start | bytes 32768 | tf_op jit(solution)/shard_map/all_to_all | solution.py:33
